TPU v7x, 32 devices: a whole 2x2x4 slice. The times are simulated.
32 devices in a mesh: group: 2 (over x), ctx: 16 (over z, y, core).
Axes of the slice: x: 2, y: 2, z: 4, core: 2. Of those that a mesh axis runs over, the one named last changes fastest.
Arguments:
- normed_hidden: bfloat16 [4096, 8192], P(('group', 'ctx')), parts along dimension 0, may hold values from -6 to 6
- queries: bfloat16 [4096, 4096], P(('group', 'ctx')), parts along dimension 0, may hold values from -45 to 45
- keys: bfloat16 [4096, 512], P(('group', 'ctx')), parts along dimension 0, may hold values from -6 to 6
- value_frozen_matrix: bfloat16 [8192, 512], P('ctx'), may hold values from -0.0625 to 0.0625
- adapter_down_weight: bfloat16 [8192, 64], replicated, may hold values from -0.0625 to 0.0625
- adapter_up_weight: bfloat16 [64, 512], replicated, may hold values from -0.75 to 0.75
- block_slot_index: int32 [64], P(('group', 'ctx')), parts along dimension 0, may hold values from 0 to 31, each once
Outputs:
- attended: bfloat16 [4096, 4096], P(('group', 'ctx')), parts along dimension 0
There are 2 independent parts, one for each index of `group`. A program takes and returns all parts, laid end to end along the dimension named above; an argument that names none is the same for every part. Nothing has to cross between parts.
Inputs may be any that keep to these rules, and one draw needn't show every extreme that they name: `block_slot_index`: each of the 32 blocks is named once; slot j holds rows j*64 to (j+1)*64 - 1.
All inputs are finite; a program needn't handle non-finite values.
Results may differ from a plain program's by a relative error of at most 0.0054.
Values may be sent and summed in bfloat16 or wider, within the bound.
No kernel may reach another device: no remote copies, remote signals or barrier semaphores. Data moves between devices by JAX's collectives and lax.ppermute only.
A program may use at most 192 MiB of HBM per device.

v0:
```python
import jax
import jax.numpy as jnp
from jax import lax
from jax.sharding import PartitionSpec as P

QH = 32
KVH = 4
HD = 128
BLK = 64


def shards(
    normed_hidden,
    queries,
    keys,
    value_frozen_matrix,
    adapter_down_weight,
    adapter_up_weight,
    block_slot_index,
):
    tokens = normed_hidden.shape[0]
    scale = 1.0 / HD**0.5
    offsets = jnp.arange(BLK, dtype=jnp.int32)
    table = lax.all_gather(block_slot_index, "ctx", axis=0, tiled=True)
    my_pos = (block_slot_index[:, None] * BLK + offsets[None, :]).reshape(tokens)
    frozen_output = jnp.dot(
        normed_hidden,
        lax.all_gather(value_frozen_matrix, "ctx", axis=0, tiled=True),
        preferred_element_type=jnp.float32,
    )
    low_rank_output = jnp.dot(
        normed_hidden, adapter_down_weight, preferred_element_type=jnp.float32
    ).astype(jnp.bfloat16)
    value_output = (
        frozen_output
        + 0.5 * jnp.dot(low_rank_output, adapter_up_weight, preferred_element_type=jnp.float32)
    ).astype(jnp.bfloat16)
    slots_here = tokens // BLK
    query_slots = [
        queries[which * BLK : (which + 1) * BLK].reshape(BLK, KVH, QH // KVH, HD)
        for which in range(slots_here)
    ]
    pos_slots = [my_pos[which * BLK : (which + 1) * BLK] for which in range(slots_here)]
    shape_stat = (KVH, QH // KVH, BLK)
    init = tuple(
        (
            (
                jnp.full(shape_stat, -1e30, jnp.float32),
                jnp.zeros(shape_stat, jnp.float32),
                jnp.zeros(shape_stat + (HD,), jnp.float32),
            )
            for which in range(slots_here)
        )
    )
    key_piece = lax.all_gather(keys, "ctx", axis=0, tiled=True)
    count = key_piece.shape[0]
    key_pos = (table[:, None] * BLK + offsets[None, :]).reshape(count)
    key_three = key_piece.reshape(count, KVH, HD)
    value_three = lax.all_gather(value_output, "ctx", axis=0, tiled=True).reshape(count, KVH, HD)
    lowest_key = jnp.min(key_pos)
    updated = []
    for attend_which in range(slots_here):
        q_part = query_slots[attend_which]
        q_pos = pos_slots[attend_which]

        def update(state, q_part=q_part, q_pos=q_pos):
            top, total, accum = state
            scores = (
                jnp.einsum("tkgd,skd->kgts", q_part, key_three, preferred_element_type=jnp.float32)
                * scale
            )
            visible = (q_pos[:, None] >= key_pos[None, :])[None, None]
            scores = jnp.where(visible, scores, -1e30)
            top_new = jnp.maximum(top, jnp.max(scores, axis=-1))
            weights = jnp.where(visible, jnp.exp(scores - top_new[..., None]), 0.0)
            total = jnp.sum(weights, axis=-1)
            accum = jnp.einsum(
                "kgts,skd->kgtd",
                weights.astype(jnp.bfloat16),
                value_three,
                preferred_element_type=jnp.float32,
            )
            return (top_new, total, accum)

        def keep(state):
            return state

        updated.append(lax.cond(lowest_key <= jnp.max(q_pos), update, keep, init[attend_which]))
    states = tuple(updated)
    outputs = []
    for which in range(slots_here):
        result = states[which][2] / states[which][1][..., None]
        outputs.append(
            jnp.transpose(result, (2, 0, 1, 3)).reshape(BLK, QH * HD).astype(jnp.bfloat16)
        )
    return jnp.concatenate(outputs, axis=0)


def solution(mesh):
    in_specs = (
        P(("group", "ctx"), None),
        P(("group", "ctx"), None),
        P(("group", "ctx"), None),
        P("ctx", None),
        P(),
        P(),
        P(("group", "ctx")),
    )
    out_specs = P(("group", "ctx"), None)
    return jax.shard_map(shards, mesh=mesh, in_specs=in_specs, out_specs=out_specs, check_vma=False)
```

profile of v0, /device:TPU:0, one launch (start us, length us, event | category | flops | bytes accessed | tf_op | source)
XLA Modules:
  0.0 216.8 jit_solution(570349210918793714)
XLA Ops:
  6.6 0.7 all-gather.6.cloned.1.call-update
  7.3 79.2 %all-gather.6.cloned.1.call-done = bf16[8192,512]{1,0:T(8,128)(2,1)} async-done(((bf16[512,512]{1,0:T(8,128)(2,1)}), bf16[8192,512]{1,0:T(8,128)(2,1)}) %all-gather.6.cloned.1.call-update) | async-done | bytes 8388624 | tf_op jit(solution)/shard_map/all_gather | solution.py:28
  86.6 4.6 %fusion.31 = f32[128,512]{1,0:T(8,128)S(1)} fusion(bf16[128,8192]{1,0:T(8,128)(2,1)S(1)} %copy-done, bf16[8192,512]{1,0:T(8,128)(2,1)} %all-gather.6.cloned.1.call-done), kind=kOutput, calls=%fused_computation.52 | convolution fusion | flops 1073741824 | bytes 10747904 | tf_op jit(solution)/shard_map/dot_general | solution.py:26
  91.2 2.4 %fusion.27 = bf16[128,512]{1,0:T(8,128)(2,1)} fusion(f32[128,512]{1,0:T(8,128)S(1)} %fusion.31, bf16[64,512]{1,0:T(8,128)(2,1)} %param.16, bf16[128,8192]{1,0:T(8,128)(2,1)S(1)} %copy-done, bf16[8192,64]{0,1:T(8,128)(2,1)S(1)} %copy-done.3), kind=kOutput, calls=%fused_computation.36 | convolution fusion | flops 142811136 | bytes 3604480 | tf_op jit(solution)/shard_map/dot_general | solution.py:36
  93.7 0.8 copy.14
  95.9 9.9 %all-reduce = s32[32]{0:T(128)S(1)} all-reduce(s32[32]{0:T(128)S(1)} %dynamic-update-slice), channel_id=1, replica_groups=mesh['group'=2,'ctx'=16] {'ctx'}, use_global_device_ids=true, to_apply=%add | all-reduce | flops 32 | bytes 256
  105.9 0.7 slice_reduce_fusion.1
  106.6 0.7 iota_add_fusion
  109.7 24.1 %all-gather.8.cloned.1.call-done = bf16[2048,512]{1,0:T(8,128)(2,1)} async-done(((bf16[128,512]{1,0:T(8,128)(2,1)}), bf16[2048,512]{1,0:T(8,128)(2,1)}) %all-gather.8.cloned.1.call-update) | async-done | bytes 2097168 | tf_op jit(solution)/shard_map/all_gather | solution.py:59
  133.7 4.0 %reshape.101 = bf16[2048,4,128]{2,1,0:T(4,128)(2,1)} reshape(bf16[2048,512]{1,0:T(8,128)(2,1)} %all-gather.8.cloned.1.call-done) | data formatting | bytes 4194304 | tf_op jit(solution)/shard_map/reshape | solution.py:59
  137.7 38.0 %all-gather.4.cloned.1.call-done = bf16[2048,512]{0,1:T(8,128)(2,1)} async-done(((bf16[128,512]{0,1:T(8,128)(2,1)}), bf16[2048,512]{0,1:T(8,128)(2,1)}) %all-gather.4.cloned.1.call-update) | async-done | bytes 2097168 | tf_op jit(solution)/shard_map/all_gather | solution.py:55
  175.7 14.9 %conditional.2 = (f32[4,8,64]{2,1,0:T(8,128)S(1)}, f32[4,8,64,128]{3,2,1,0:T(8,128)S(1)}) conditional(s32[]{:T(128)} %convert_element_type.36, () %tuple.21, (s32[1,64]{1,0:T(1,128)S(1)}, s32[32,64]{1,0:T(8,128)S(1)}, bf16[128,4096]{1,0:T(8,128)(2,1)}, bf16[2048,4,128]{0,2,1:T(8,128)(2,1)}, bf16[2048,4,128]{2,1,0:T(4,128)(2,1)}) %tuple.46), branch_computations={%region_2.0_spmd, %region_3.6_spmd} | conditional | flops 2202138624 | bytes 67182896 | solution.py:88
  175.9 1.2 slice_bitcast_fusion
  177.2 4.4 %fusion = (f32[4,8,64]{2,1,0:T(8,128)S(1)}, f32[4,2048,64,8]{1,2,3,0:T(8,128)S(1)}) fusion(pred[64,2048]{1,0:T(8,128)(4,1)S(1)} %broadcast_compare_fusion, bf16[64,4,8,128]{3,2,1,0:T(8,128)(2,1)S(1)} %bitcast.69, bf16[2048,4,128]{0,2,1:T(8,128)(2,1)} %get-tuple-element.62), kind=kOutput, calls=%fused_computation.2 | convolution fusion | flops 1086322688 | bytes 19537920 | tf_op jit(solution)/shard_map/cond/branch_1_fun/tkgd,skd->kgts/dot_general | solution.py:69
  181.7 3.8 %fusion.3 = f32[4,8,64,128]{3,2,1,0:T(8,128)S(1)} fusion(f32[4,2048,64,8]{1,2,3,0:T(8,128)S(1)} %get-tuple-element.72, f32[4,8,64]{2,1,0:T(8,128)S(1)} %broadcast_maximum_fusion, pred[64,2048]{1,0:T(8,128)(4,1)S(1)} %broadcast_compare_fusion, bf16[2048,4,128,1]{2,1,0,3:T(4,128)(2,1)S(1)} %bitcast.71), kind=kOutput, calls=%fused_computation.5 | convolution fusion | flops 1094713344 | bytes 20062208 | tf_op jit(solution)/shard_map/cond/branch_1_fun/kgts,skd->kgtd/dot_general | solution.py:77
  185.5 5.1 %fusion.2 = f32[4,8,64]{2,1,0:T(8,128)S(1)} fusion(f32[4,2048,64,8]{1,2,3,0:T(8,128)S(1)} %get-tuple-element.72, f32[4,8,64]{2,1,0:T(8,128)S(1)} %broadcast_maximum_fusion, pred[64,2048]{1,0:T(8,128)(4,1)S(1)} %broadcast_compare_fusion), kind=kLoop, calls=%fused_computation.4 | loop fusion | flops 20969472 | bytes 16924672 | tf_op jit(solution)/shard_map/cond/branch_1_fun/reduce_sum | solution.py:76
  191.0 1.1 copy.17
  192.1 14.9 %conditional.3 = (f32[4,8,64]{2,1,0:T(8,128)S(1)}, f32[4,8,64,128]{3,2,1,0:T(8,128)S(1)}) conditional(s32[]{:T(128)} %convert_element_type.42, () %tuple.23, (s32[1,64]{1,0:T(1,128)S(1)}, s32[32,64]{1,0:T(8,128)S(1)}, bf16[128,4096]{1,0:T(8,128)(2,1)}, bf16[2048,4,128]{0,2,1:T(8,128)(2,1)}, bf16[2048,4,128]{2,1,0:T(4,128)(2,1)}) %tuple.47), branch_computations={%region_7.8_spmd, %region_8.11_spmd} | conditional | flops 2202138624 | bytes 67182896 | solution.py:88
  192.3 1.2 slice_bitcast_fusion.1
  193.6 4.4 %fusion.13 = (f32[4,8,64]{2,1,0:T(8,128)S(1)}, f32[4,2048,64,8]{1,2,3,0:T(8,128)S(1)}) fusion(pred[64,2048]{1,0:T(8,128)(4,1)S(1)} %broadcast_compare_fusion.1, bf16[64,4,8,128]{3,2,1,0:T(8,128)(2,1)S(1)} %bitcast.70, bf16[2048,4,128]{0,2,1:T(8,128)(2,1)} %get-tuple-element.67), kind=kOutput, calls=%fused_computation.19 | convolution fusion | flops 1086322688 | bytes 19537920 | tf_op jit(solution)/shard_map/cond/branch_1_fun/tkgd,skd->kgts/dot_general | solution.py:69
  198.1 3.8 %fusion.16 = f32[4,8,64,128]{3,2,1,0:T(8,128)S(1)} fusion(f32[4,2048,64,8]{1,2,3,0:T(8,128)S(1)} %get-tuple-element.74, f32[4,8,64]{2,1,0:T(8,128)S(1)} %broadcast_maximum_fusion.1, pred[64,2048]{1,0:T(8,128)(4,1)S(1)} %broadcast_compare_fusion.1, bf16[2048,4,128,1]{2,1,0,3:T(4,128)(2,1)S(1)} %bitcast.72), kind=kOutput, calls=%fused_computation.22 | convolution fusion | flops 1094713344 | bytes 20062208 | tf_op jit(solution)/shard_map/cond/branch_1_fun/kgts,skd->kgtd/dot_general | solution.py:77
  202.0 5.1 %fusion.15 = f32[4,8,64]{2,1,0:T(8,128)S(1)} fusion(f32[4,2048,64,8]{1,2,3,0:T(8,128)S(1)} %get-tuple-element.74, f32[4,8,64]{2,1,0:T(8,128)S(1)} %broadcast_maximum_fusion.1, pred[64,2048]{1,0:T(8,128)(4,1)S(1)} %broadcast_compare_fusion.1), kind=kLoop, calls=%fused_computation.21 | loop fusion | flops 20969472 | bytes 16924672 | tf_op jit(solution)/shard_map/cond/branch_1_fun/reduce_sum | solution.py:76
  207.8 1.4 copy_bitcast_fusion
  209.2 1.1 pad_maximum_fusion
  (36 shorter events, 2.7 us)
Async XLA Ops:
  6.5 80.0 %copy-start = (bf16[128,8192]{1,0:T(8,128)(2,1)S(1)}, bf16[128,8192]{1,0:T(8,128)(2,1)}, u32[]{:S(2)}) copy-start(bf16[128,8192]{1,0:T(8,128)(2,1)} %param.11) | copy-start | bytes 6291460
  6.5 87.9 %copy-start.6 = (u32[32]{0:T(128)S(1)}, u32[32]{0:T(128)}, u32[]{:S(2)}) copy-start(u32[32]{0:T(128)} %constant.9) | copy-start | bytes 388
  6.5 84.7 %copy-start.3 = (bf16[8192,64]{0,1:T(8,128)(2,1)S(1)}, bf16[8192,64]{0,1:T(8,128)(2,1)}, u32[]{:S(2)}) copy-start(bf16[8192,64]{0,1:T(8,128)(2,1)} %param.15) | copy-start | bytes 3145732
  6.5 87.1 %copy-start.4 = (bf16[128,512]{1,0:T(8,128)(2,1)S(1)}, bf16[128,512]{1,0:T(8,128)(2,1)}, u32[]{:S(2)}) copy-start(bf16[128,512]{1,0:T(8,128)(2,1)} %param.13) | copy-start | bytes 393220
  6.5 89.1 %copy-start.5 = (s32[2]{0:T(128)S(1)}, s32[2]{0:T(128)}, u32[]{:S(2)}) copy-start(s32[2]{0:T(128)} %param.17) | copy-start | bytes 28
  6.5 80.0 %all-gather.6.cloned.1.call-start = ((), (), s32[]{:S(2)}) async-start(), calls=%async_computation.1 | async-start | bytes 8912896 | tf_op jit(solution)/shard_map/all_gather | solution.py:28
  7.3 126.5 %all-gather.8.cloned.1.call-start = ((), (), s32[]{:S(2)}) async-start(), calls=%async_computation.2 | async-start | bytes 2228224 | tf_op jit(solution)/shard_map/all_gather | solution.py:59
  93.6 82.1 %all-gather.4.cloned.1.call-start = ((), (), s32[]{:S(2)}) async-start(), calls=%async_computation | async-start | bytes 2228224 | tf_op jit(solution)/shard_map/all_gather | solution.py:55
  175.8 5.9 %copy-start.1 = (bf16[2048,4,128]{2,1,0:T(4,128)(2,1)S(1)}, bf16[2048,4,128]{2,1,0:T(4,128)(2,1)}, u32[]{:S(2)}) copy-start(bf16[2048,4,128]{2,1,0:T(4,128)(2,1)} %get-tuple-element.63) | copy-start | bytes 6291460 | tf_op jit(solution)/shard_map/cond
  192.2 5.9 %copy-start.2 = (bf16[2048,4,128]{2,1,0:T(4,128)(2,1)S(1)}, bf16[2048,4,128]{2,1,0:T(4,128)(2,1)}, u32[]{:S(2)}) copy-start(bf16[2048,4,128]{2,1,0:T(4,128)(2,1)} %get-tuple-element.68) | copy-start | bytes 6291460 | tf_op jit(solution)/shard_map/cond
Sparse Core Ops, SparseCore 0:
  9.5 77.0 all-gather.5
  93.7 39.9 all-gather.7
  135.9 39.7 all-gather.3
where the time goes:
time: 217 us
  waiting for transfers between devices  142 us (65%)
  matrix products  23.5 us (11%)
  between operations  16.1 us (7%)
  other arithmetic  13.7 us (6%)
  local copies, waits for them, and re-layouts  11.2 us (5%)
  blocking collectives  9.93 us (5%)
    all_gather x1, waiting for transfers between devices, shards(): lax.all_gather(value_frozen_matrix, 'ctx', axis=0, tiled=True)  79.2 us
    all_gather x1, waiting for transfers between devices, shards(): key_piece = lax.all_gather(keys, 'ctx', axis=0, tiled=True)  38 us
    all_gather x1, waiting for transfers between devices, shards(): lax.all_gather(value_output, 'ctx', axis=0, tiled=True)  24.1 us
    reduce_sum x2, other arithmetic, update(): total = jnp.sum(weights, axis=-1)  10.2 us
    unnamed x1, blocking collectives  9.93 us
    dot_general x2, matrix products, update(): jnp.einsum('tkgd,skd->kgts', q_part, key_three, preferred_element_type=jn...  8.88 us
    dot_general x2, matrix products, update(): jnp.einsum('kgts,skd->kgtd', weights.astype(jnp.bfloat16), value_three, p...  7.67 us
    dot_general x1, matrix products, shards(): jnp.dot(normed_hidden, lax.all_gather(value_frozen_matrix, 'ctx', axis=0,...  4.63 us
  transfers between devices with their start and end apart: 3, of which 3 were waited for; matrix products, arithmetic and copies ran while one was open for 3% of the time, Pallas kernels for 0%

commit v1 on v0

--- a/solution.py
+++ b/solution.py
@@ -23,9 +23,38 @@
     offsets = jnp.arange(BLK, dtype=jnp.int32)
     table = lax.all_gather(block_slot_index, "ctx", axis=0, tiled=True)
     my_pos = (block_slot_index[:, None] * BLK + offsets[None, :]).reshape(tokens)
+
+    def pairs_all_plan(block_here, group_axis):
+        q_next, tmp, x_next = (
+            lax.psum(1, axis_name=group_axis),
+            lax.axis_index(group_axis),
+            block_here.shape[0],
+        )
+        rows = [(src_i, (src_i + 1) % q_next) for src_i in range(q_next)]
+        pool = [(src_i, (src_i - 1) % q_next) for src_i in range(q_next)]
+        mixed_arr = jnp.zeros(
+            (*block_here.shape[:0], q_next * x_next, *block_here.shape[1:]), block_here.dtype
+        )
+        mixed_arr = lax.dynamic_update_slice_in_dim(mixed_arr, block_here, tmp * x_next, axis=0)
+        arr_out = mid_arr = block_here
+        arr_now = q_next // 2
+        jj = 1
+        while jj < arr_now + 1:
+            arr_out = lax.ppermute(arr_out, axis_name=group_axis, perm=rows)
+            mixed_arr = lax.dynamic_update_slice_in_dim(
+                mixed_arr, arr_out, (tmp - jj) % q_next * x_next, axis=0
+            )
+            if jj < q_next - arr_now:
+                mid_arr = lax.ppermute(mid_arr, axis_name=group_axis, perm=pool)
+                mixed_arr = lax.dynamic_update_slice_in_dim(
+                    mixed_arr, mid_arr, (tmp + jj) % q_next * x_next, axis=0
+                )
+            jj += 1
+        return mixed_arr
+
     frozen_output = jnp.dot(
         normed_hidden,
-        lax.all_gather(value_frozen_matrix, "ctx", axis=0, tiled=True),
+        pairs_all_plan(value_frozen_matrix, "ctx"),
         preferred_element_type=jnp.float32,
     )
     low_rank_output = jnp.dot(

time: 217 us -> 209 us (0.963)
  waiting for transfers between devices: 142 us -> 53.5 us
  starting transfers between devices: 0.12 us -> 52.3 us
  local copies, waits for them, and re-layouts: 11.2 us -> 33.5 us
  blocking collectives: 9.93 us -> 14.2 us
    all_gather x1 -> x0, waiting for transfers between devices: 79.2 us -> none  [shards(): lax.all_gather(value_frozen_matrix, 'ctx', axis=0, tiled=True)]
    ppermute x0 -> x15, starting transfers between devices: none -> 52.3 us  [the longest x8 42.1 us: pairs_all_plan(): arr_out = lax.ppermute(arr_out, axis_name=group_axis, perm=rows)]
    all_gather x1, waiting for transfers between devices: 38 us -> 0.02 us  [shards(): key_piece = lax.all_gather(keys, 'ctx', axis=0, tiled=True)]
    ppermute x0 -> x15, waiting for transfers between devices: none -> 28.1 us  [the longest x8 28.1 us: pairs_all_plan(): arr_out = lax.ppermute(arr_out, axis_name=group_axis, perm=rows)]
    dynamic_update_slice x0 -> x16, local copies, waits for them, and re-layouts: none -> 23.8 us  [the longest x8 11.9 us: pairs_all_plan(): lax.dynamic_update_slice_in_dim(mixed_arr, arr_out, (tmp - jj) % q_next *...]
    unnamed x1, blocking collectives: 9.93 us -> 14.2 us
    reshape x1 -> x0, local copies, waits for them, and re-layouts: 3.96 us -> none  [shards(): lax.all_gather(value_output, 'ctx', axis=0, tiled=True)]
    broadcast_in_dim x0 -> x1, local copies, waits for them, and re-layouts: none -> 3.76 us  [pairs_all_plan(): jnp.zeros((*block_here.shape[:0], q_next * x_next, *block_here.shape[1:])...]
  transfers between devices with their start and end apart: 3 -> 17, of which waited for: 3 -> 6; matrix products, arithmetic and copies ran while one was open for 3% -> 19% of each run, Pallas kernels for 0% -> 0%
where the time goes in v1:
time: 209 us
  waiting for transfers between devices  53.5 us (26%)
  starting transfers between devices  52.3 us (25%)
  local copies, waits for them, and re-layouts  33.5 us (16%)
  matrix products  24.9 us (12%)
  between operations  16.5 us (8%)
  blocking collectives  14.2 us (7%)
  other arithmetic  13.6 us (7%)
    ppermute x8, starting transfers between devices, pairs_all_plan(): arr_out = lax.ppermute(arr_out, axis_name=group_axis, perm=rows)  42.1 us
    ppermute x8, waiting for transfers between devices, pairs_all_plan(): arr_out = lax.ppermute(arr_out, axis_name=group_axis, perm=rows)  28.1 us
    all_gather x1, waiting for transfers between devices, shards(): lax.all_gather(value_output, 'ctx', axis=0, tiled=True)  25.4 us
    unnamed x1, blocking collectives  14.2 us
    dynamic_update_slice x8, local copies, waits for them, and re-layouts, pairs_all_plan(): lax.dynamic_update_slice_in_dim(mixed_arr, arr_out, (tmp - jj) % q_next *...  11.9 us
    dynamic_update_slice x7, local copies, waits for them, and re-layouts, pairs_all_plan(): lax.dynamic_update_slice_in_dim(mixed_arr, mid_arr, (tmp + jj) % q_next *...  11.1 us
    ppermute x7, starting transfers between devices, pairs_all_plan(): mid_arr = lax.ppermute(mid_arr, axis_name=group_axis, perm=pool)  10.2 us
    reduce_sum x2, other arithmetic, update(): total = jnp.sum(weights, axis=-1)  10.1 us
  transfers between devices with their start and end apart: 17, of which 6 were waited for; matrix products, arithmetic and copies ran while one was open for 19% of the time, Pallas kernels for 0%

profile of v1, /device:TPU:0, one launch (start us, length us, event | category | flops | bytes accessed | tf_op | source)
XLA Modules:
  0.0 208.7 jit_solution(11177010414360955388)
XLA Ops:
  7.0 5.0 %collective-permute-start.1 = (bf16[512,512]{1,0:T(8,128)(2,1)}, bf16[512,512]{1,0:T(8,128)(2,1)}, u32[]{:S(2)}, u32[]{:S(2)}) collective-permute-start(bf16[512,512]{1,0:T(8,128)(2,1)} %param.14), channel_id=1, source_target_pairs={{0,15},{1,0},{2,1},{3,2},{4,3},{5,4},{6,5},{7,6},{8,7},{9,8},{10,9... | collective-permute-start | bytes 1572872 | tf_op jit(solution)/shard_map/ppermute | solution.py:48
  12.1 7.2 %collective-permute-done = bf16[512,512]{1,0:T(8,128)(2,1)} collective-permute-done((bf16[512,512]{1,0:T(8,128)(2,1)}, bf16[512,512]{1,0:T(8,128)(2,1)}, u32[]{:S(2)}, u32[]{:S(2)}) %collective-permute-start) | collective-permute-done | bytes 524320 | tf_op jit(solution)/shard_map/ppermute | solution.py:43
  23.8 7.2 %collective-permute-done.2 = bf16[512,512]{1,0:T(8,128)(2,1)} collective-permute-done((bf16[512,512]{1,0:T(8,128)(2,1)}, bf16[512,512]{1,0:T(8,128)(2,1)}, u32[]{:S(2)}, u32[]{:S(2)}) %collective-permute-start.2) | collective-permute-done | bytes 524320 | tf_op jit(solution)/shard_map/ppermute | solution.py:43
  31.0 4.4 %collective-permute-start.4 = (bf16[512,512]{1,0:T(8,128)(2,1)}, bf16[512,512]{1,0:T(8,128)(2,1)S(1)}, u32[]{:S(2)}, u32[]{:S(2)}) collective-permute-start(bf16[512,512]{1,0:T(8,128)(2,1)} %collective-permute-done.2), channel_id=1, source_target_pairs={{0,1},{1,2},{2,3},{3,4},{4,5},{5,6},{6,7},{7,8},{8,9},{9,10},{10,1... | collective-permute-start | bytes 1572872 | tf_op jit(solution)/shard_map/ppermute | solution.py:43
  35.5 7.1 %collective-permute-done.4 = bf16[512,512]{1,0:T(8,128)(2,1)S(1)} collective-permute-done((bf16[512,512]{1,0:T(8,128)(2,1)}, bf16[512,512]{1,0:T(8,128)(2,1)S(1)}, u32[]{:S(2)}, u32[]{:S(2)}) %collective-permute-start.4) | collective-permute-done | bytes 524320 | tf_op jit(solution)/shard_map/ppermute | solution.py:43
  42.7 6.6 %collective-permute-start.6 = (bf16[512,512]{1,0:T(8,128)(2,1)S(1)}, bf16[512,512]{1,0:T(8,128)(2,1)}, u32[]{:S(2)}, u32[]{:S(2)}) collective-permute-start(bf16[512,512]{1,0:T(8,128)(2,1)S(1)} %collective-permute-done.4), channel_id=1, source_target_pairs={{0,1},{1,2},{2,3},{3,4},{4,5},{5,6},{6,7},{7,8},{8,9},{9,10},{10,1... | collective-permute-start | bytes 1572872 | tf_op jit(solution)/shard_map/ppermute | solution.py:43
  51.1 3.0 %collective-permute-done.6 = bf16[512,512]{1,0:T(8,128)(2,1)} collective-permute-done((bf16[512,512]{1,0:T(8,128)(2,1)S(1)}, bf16[512,512]{1,0:T(8,128)(2,1)}, u32[]{:S(2)}, u32[]{:S(2)}) %collective-permute-start.6) | collective-permute-done | bytes 524320 | tf_op jit(solution)/shard_map/ppermute | solution.py:43
  54.1 10.7 %collective-permute-start.8 = (bf16[512,512]{1,0:T(8,128)(2,1)}, bf16[512,512]{1,0:T(8,128)(2,1)}, u32[]{:S(2)}, u32[]{:S(2)}) collective-permute-start(bf16[512,512]{1,0:T(8,128)(2,1)} %collective-permute-done.6), channel_id=1, source_target_pairs={{0,1},{1,2},{2,3},{3,4},{4,5},{5,6},{6,7},{7,8},{8,9},{9,10},{10,1... | collective-permute-start | bytes 1572872 | tf_op jit(solution)/shard_map/ppermute | solution.py:43
  67.0 11.8 %collective-permute-start.10 = (bf16[512,512]{1,0:T(8,128)(2,1)}, bf16[512,512]{1,0:T(8,128)(2,1)}, u32[]{:S(2)}, u32[]{:S(2)}) collective-permute-start(bf16[512,512]{1,0:T(8,128)(2,1)} %collective-permute-done.8), channel_id=1, source_target_pairs={{0,1},{1,2},{2,3},{3,4},{4,5},{5,6},{6,7},{7,8},{8,9},{9,10},{10,1... | collective-permute-start | bytes 1572872 | tf_op jit(solution)/shard_map/ppermute | solution.py:43
  78.8 3.8 %broadcast_in_dim.47 = bf16[8192,512]{1,0:T(8,128)(2,1)} broadcast(bf16[]{:T(256)} %constant.121.clone.1), dimensions={} | broadcast | bytes 8388610 | tf_op jit(solution)/shard_map/broadcast_in_dim | solution.py:35
  91.0 3.0 %collective-permute-start.12 = (bf16[512,512]{1,0:T(8,128)(2,1)}, bf16[512,512]{1,0:T(8,128)(2,1)S(1)}, u32[]{:S(2)}, u32[]{:S(2)}) collective-permute-start(bf16[512,512]{1,0:T(8,128)(2,1)} %collective-permute-done.10), channel_id=1, source_target_pairs={{0,1},{1,2},{2,3},{3,4},{4,5},{5,6},{6,7},{7,8},{8,9},{9,10},{10,1... | collective-permute-start | bytes 1572872 | tf_op jit(solution)/shard_map/ppermute | solution.py:43
  100.4 3.0 %collective-permute-start.13 = (bf16[512,512]{1,0:T(8,128)(2,1)S(1)}, bf16[512,512]{1,0:T(8,128)(2,1)S(1)}, u32[]{:S(2)}, u32[]{:S(2)}) collective-permute-start(bf16[512,512]{1,0:T(8,128)(2,1)S(1)} %collective-permute-done.11), channel_id=1, source_target_pairs={{0,15},{1,0},{2,1},{3,2},{4,3},{5,4},{6,5},{7,6},{8,7},{9,8},{10,9... | collective-permute-start | bytes 1572872 | tf_op jit(solution)/shard_map/ppermute | solution.py:48
  114.2 3.5 %collective-permute-done.14 = bf16[512,512]{1,0:T(8,128)(2,1)S(1)} collective-permute-done((bf16[512,512]{1,0:T(8,128)(2,1)S(1)}, bf16[512,512]{1,0:T(8,128)(2,1)S(1)}, u32[]{:S(2)}, u32[]{:S(2)}) %collective-permute-start.14) | collective-permute-done | bytes 524320 | tf_op jit(solution)/shard_map/ppermute | solution.py:43
  118.5 6.5 %fusion.27 = bf16[128,512]{0,1:T(8,128)(2,1)} fusion(f32[128,512]{0,1:T(8,128)S(1)} %convolution_multiply_fusion, bf16[8192,512]{1,0:T(8,128)(2,1)} %constant_dynamic-update-slice_fusion, bf16[128,8192]{1,0:T(8,128)(2,1)S(1)} %copy-done), kind=kOutput, calls=%fused_computation.37 | convolution fusion | flops 1073872896 | bytes 10878976 | tf_op jit(solution)/shard_map/dot_general | solution.py:55
  126.5 14.2 %all-reduce = s32[32]{0:T(128)S(1)} all-reduce(s32[32]{0:T(128)S(1)} %dynamic-update-slice), channel_id=1, replica_groups=mesh['group'=2,'ctx'=16] {'ctx'}, use_global_device_ids=true, to_apply=%add | all-reduce | flops 32 | bytes 256
  144.6 25.4 %all-gather.5.cloned.1.call-done = bf16[2048,512]{0,1:T(8,128)(2,1)} async-done(((bf16[128,512]{0,1:T(8,128)(2,1)}), bf16[2048,512]{0,1:T(8,128)(2,1)}) %all-gather.5.cloned.1.call-update) | async-done | bytes 2097168 | tf_op jit(solution)/shard_map/all_gather | solution.py:88
  170.0 13.6 %conditional.2 = (f32[4,8,64]{2,1,0:T(8,128)S(1)}, f32[4,8,64,128]{3,2,1,0:T(8,128)S(1)}) conditional(s32[]{:T(128)} %convert_element_type.36, () %tuple.21, (s32[1,64]{1,0:T(1,128)S(1)}, s32[32,64]{1,0:T(8,128)S(1)}, bf16[128,4096]{1,0:T(8,128)(2,1)S(1)}, bf16[2048,4,128]{0,2,1:T(8,128)(2,1)}, bf16[2048,4,128]{0,2,1:T(8,128)(2,1)}) %tuple.48), branch_computations={%region_2.3_spmd, %region_3.6_spmd} | conditional | flops 2202138624 | bytes 67182896 | solution.py:117
  170.3 4.6 %fusion = (f32[4,8,64]{2,1,0:T(8,128)S(1)}, f32[4,2048,64,8]{1,2,3,0:T(8,128)S(1)}) fusion(pred[64,2048]{1,0:T(8,128)(4,1)S(1)} %broadcast_compare_fusion, bf16[64,4,8,128]{3,2,1,0:T(8,128)(2,1)S(1)} %bitcast.84, bf16[2048,4,128]{0,2,1:T(8,128)(2,1)} %get-tuple-element.62), kind=kOutput, calls=%fused_computation.2 | convolution fusion | flops 1086322688 | bytes 19537920 | tf_op jit(solution)/shard_map/cond/branch_1_fun/tkgd,skd->kgts/dot_general | solution.py:98
  174.9 3.5 %fusion.3 = f32[4,8,64,128]{3,2,1,0:T(8,128)S(1)} fusion(f32[4,2048,64,8]{1,2,3,0:T(8,128)S(1)} %get-tuple-element.72, f32[4,8,64]{2,1,0:T(8,128)S(1)} %broadcast_maximum_fusion, pred[64,2048]{1,0:T(8,128)(4,1)S(1)} %broadcast_compare_fusion, bf16[2048,4,128]{0,2,1:T(8,128)(2,1)S(1)} %copy-done.4), kind=kOutput, calls=%fused_computation.5 | convolution fusion | flops 1094713344 | bytes 20062208 | tf_op jit(solution)/shard_map/cond/branch_1_fun/kgts,skd->kgtd/dot_general | solution.py:106
  178.5 5.1 %fusion.2 = f32[4,8,64]{2,1,0:T(8,128)S(1)} fusion(f32[4,2048,64,8]{1,2,3,0:T(8,128)S(1)} %get-tuple-element.72, f32[4,8,64]{2,1,0:T(8,128)S(1)} %broadcast_maximum_fusion, pred[64,2048]{1,0:T(8,128)(4,1)S(1)} %broadcast_compare_fusion), kind=kLoop, calls=%fused_computation.4 | loop fusion | flops 20969472 | bytes 16924672 | tf_op jit(solution)/shard_map/cond/branch_1_fun/reduce_sum | solution.py:105
  185.0 13.6 %conditional.3 = (f32[4,8,64]{2,1,0:T(8,128)S(1)}, f32[4,8,64,128]{3,2,1,0:T(8,128)S(1)}) conditional(s32[]{:T(128)} %convert_element_type.42, () %tuple.23, (s32[1,64]{1,0:T(1,128)S(1)}, s32[32,64]{1,0:T(8,128)S(1)}, bf16[128,4096]{1,0:T(8,128)(2,1)S(1)}, bf16[2048,4,128]{0,2,1:T(8,128)(2,1)}, bf16[2048,4,128]{0,2,1:T(8,128)(2,1)}) %tuple.49), branch_computations={%region_7.8_spmd, %region_8.11_spmd} | conditional | flops 2202138624 | bytes 67182896 | solution.py:117
  185.4 4.6 %fusion.13 = (f32[4,8,64]{2,1,0:T(8,128)S(1)}, f32[4,2048,64,8]{1,2,3,0:T(8,128)S(1)}) fusion(pred[64,2048]{1,0:T(8,128)(4,1)S(1)} %broadcast_compare_fusion.1, bf16[64,4,8,128]{3,2,1,0:T(8,128)(2,1)S(1)} %bitcast.85, bf16[2048,4,128]{0,2,1:T(8,128)(2,1)} %get-tuple-element.67), kind=kOutput, calls=%fused_computation.19 | convolution fusion | flops 1086322688 | bytes 19537920 | tf_op jit(solution)/shard_map/cond/branch_1_fun/tkgd,skd->kgts/dot_general | solution.py:98
  190.0 3.5 %fusion.16 = f32[4,8,64,128]{3,2,1,0:T(8,128)S(1)} fusion(f32[4,2048,64,8]{1,2,3,0:T(8,128)S(1)} %get-tuple-element.74, f32[4,8,64]{2,1,0:T(8,128)S(1)} %broadcast_maximum_fusion.1, pred[64,2048]{1,0:T(8,128)(4,1)S(1)} %broadcast_compare_fusion.1, bf16[2048,4,128]{0,2,1:T(8,128)(2,1)S(1)} %copy-done.5), kind=kOutput, calls=%fused_computation.22 | convolution fusion | flops 1094713344 | bytes 20062208 | tf_op jit(solution)/shard_map/cond/branch_1_fun/kgts,skd->kgtd/dot_general | solution.py:106
  193.6 5.1 %fusion.15 = f32[4,8,64]{2,1,0:T(8,128)S(1)} fusion(f32[4,2048,64,8]{1,2,3,0:T(8,128)S(1)} %get-tuple-element.74, f32[4,8,64]{2,1,0:T(8,128)S(1)} %broadcast_maximum_fusion.1, pred[64,2048]{1,0:T(8,128)(4,1)S(1)} %broadcast_compare_fusion.1), kind=kLoop, calls=%fused_computation.21 | loop fusion | flops 20969472 | bytes 16924672 | tf_op jit(solution)/shard_map/cond/branch_1_fun/reduce_sum | solution.py:105
  (81 shorter events, 43.1 us)
Async XLA Ops:
  6.5 58.3 %copy-start = (bf16[128,8192]{1,0:T(8,128)(2,1)S(1)}, bf16[128,8192]{1,0:T(8,128)(2,1)}, u32[]{:S(2)}) copy-start(bf16[128,8192]{1,0:T(8,128)(2,1)} %param.11) | copy-start | bytes 6291460
  6.5 76.0 %copy-start.3 = (bf16[512,512]{1,0:T(8,128)(2,1)S(1)}, bf16[512,512]{1,0:T(8,128)(2,1)}, u32[]{:S(2)}) copy-start(bf16[512,512]{1,0:T(8,128)(2,1)} %param.14) | copy-start | bytes 1572868
  6.5 138.1 %all-gather.3.cloned.1.call-start = ((), (), s32[]{:S(2)}) async-start(), calls=%async_computation | async-start | bytes 2228224 | tf_op jit(solution)/shard_map/all_gather | solution.py:84
  6.5 12.8 %collective-permute-start = (bf16[512,512]{1,0:T(8,128)(2,1)}, bf16[512,512]{1,0:T(8,128)(2,1)}, u32[]{:S(2)}, u32[]{:S(2)}) collective-permute-start(bf16[512,512]{1,0:T(8,128)(2,1)} %param.14), channel_id=1, source_target_pairs={{0,1},{1,2},{2,3},{3,4},{4,5},{5,6},{6,7},{7,8},{8,9},{9,10},{10,1... | collective-permute-start | bytes 1572872 | tf_op jit(solution)/shard_map/ppermute | solution.py:43
  7.0 14.7 %collective-permute-start.1 = (bf16[512,512]{1,0:T(8,128)(2,1)}, bf16[512,512]{1,0:T(8,128)(2,1)}, u32[]{:S(2)}, u32[]{:S(2)}) collective-permute-start(bf16[512,512]{1,0:T(8,128)(2,1)} %param.14), channel_id=1, source_target_pairs={{0,15},{1,0},{2,1},{3,2},{4,3},{5,4},{6,5},{7,6},{8,7},{9,8},{10,9... | collective-permute-start | bytes 1572872 | tf_op jit(solution)/shard_map/ppermute | solution.py:48
  19.3 11.7 %collective-permute-start.2 = (bf16[512,512]{1,0:T(8,128)(2,1)}, bf16[512,512]{1,0:T(8,128)(2,1)}, u32[]{:S(2)}, u32[]{:S(2)}) collective-permute-start(bf16[512,512]{1,0:T(8,128)(2,1)} %collective-permute-done), channel_id=1, source_target_pairs={{0,1},{1,2},{2,3},{3,4},{4,5},{5,6},{6,7},{7,8},{8,9},{9,10},{10,1... | collective-permute-start | bytes 1572872 | tf_op jit(solution)/shard_map/ppermute | solution.py:43
  21.7 13.8 %collective-permute-start.3 = (bf16[512,512]{1,0:T(8,128)(2,1)}, bf16[512,512]{1,0:T(8,128)(2,1)}, u32[]{:S(2)}, u32[]{:S(2)}) collective-permute-start(bf16[512,512]{1,0:T(8,128)(2,1)} %collective-permute-done.1), channel_id=1, source_target_pairs={{0,15},{1,0},{2,1},{3,2},{4,3},{5,4},{6,5},{7,6},{8,7},{9,8},{10,9... | collective-permute-start | bytes 1572872 | tf_op jit(solution)/shard_map/ppermute | solution.py:48
  31.0 11.6 %collective-permute-start.4 = (bf16[512,512]{1,0:T(8,128)(2,1)}, bf16[512,512]{1,0:T(8,128)(2,1)S(1)}, u32[]{:S(2)}, u32[]{:S(2)}) collective-permute-start(bf16[512,512]{1,0:T(8,128)(2,1)} %collective-permute-done.2), channel_id=1, source_target_pairs={{0,1},{1,2},{2,3},{3,4},{4,5},{5,6},{6,7},{7,8},{8,9},{9,10},{10,1... | collective-permute-start | bytes 1572872 | tf_op jit(solution)/shard_map/ppermute | solution.py:43
  35.5 15.5 %collective-permute-start.5 = (bf16[512,512]{1,0:T(8,128)(2,1)}, bf16[512,512]{1,0:T(8,128)(2,1)}, u32[]{:S(2)}, u32[]{:S(2)}) collective-permute-start(bf16[512,512]{1,0:T(8,128)(2,1)} %collective-permute-done.3), channel_id=1, source_target_pairs={{0,15},{1,0},{2,1},{3,2},{4,3},{5,4},{6,5},{7,6},{8,7},{9,8},{10,9... | collective-permute-start | bytes 1572872 | tf_op jit(solution)/shard_map/ppermute | solution.py:48
  42.7 11.4 %collective-permute-start.6 = (bf16[512,512]{1,0:T(8,128)(2,1)S(1)}, bf16[512,512]{1,0:T(8,128)(2,1)}, u32[]{:S(2)}, u32[]{:S(2)}) collective-permute-start(bf16[512,512]{1,0:T(8,128)(2,1)S(1)} %collective-permute-done.4), channel_id=1, source_target_pairs={{0,1},{1,2},{2,3},{3,4},{4,5},{5,6},{6,7},{7,8},{8,9},{9,10},{10,1... | collective-permute-start | bytes 1572872 | tf_op jit(solution)/shard_map/ppermute | solution.py:43
  50.9 119.0 %all-gather.5.cloned.1.call-start = ((), (), s32[]{:S(2)}) async-start(), calls=%async_computation.1 | async-start | bytes 2228224 | tf_op jit(solution)/shard_map/all_gather | solution.py:88
  51.0 13.8 %collective-permute-start.7 = (bf16[512,512]{1,0:T(8,128)(2,1)}, bf16[512,512]{1,0:T(8,128)(2,1)}, u32[]{:S(2)}, u32[]{:S(2)}) collective-permute-start(bf16[512,512]{1,0:T(8,128)(2,1)} %collective-permute-done.5), channel_id=1, source_target_pairs={{0,15},{1,0},{2,1},{3,2},{4,3},{5,4},{6,5},{7,6},{8,7},{9,8},{10,9... | collective-permute-start | bytes 1572872 | tf_op jit(solution)/shard_map/ppermute | solution.py:48
  54.1 12.9 %collective-permute-start.8 = (bf16[512,512]{1,0:T(8,128)(2,1)}, bf16[512,512]{1,0:T(8,128)(2,1)}, u32[]{:S(2)}, u32[]{:S(2)}) collective-permute-start(bf16[512,512]{1,0:T(8,128)(2,1)} %collective-permute-done.6), channel_id=1, source_target_pairs={{0,1},{1,2},{2,3},{3,4},{4,5},{5,6},{6,7},{7,8},{8,9},{9,10},{10,1... | collective-permute-start | bytes 1572872 | tf_op jit(solution)/shard_map/ppermute | solution.py:43
  64.8 24.3 %collective-permute-start.9 = (bf16[512,512]{1,0:T(8,128)(2,1)}, bf16[512,512]{1,0:T(8,128)(2,1)}, u32[]{:S(2)}, u32[]{:S(2)}) collective-permute-start(bf16[512,512]{1,0:T(8,128)(2,1)} %collective-permute-done.7), channel_id=1, source_target_pairs={{0,15},{1,0},{2,1},{3,2},{4,3},{5,4},{6,5},{7,6},{8,7},{9,8},{10,9... | collective-permute-start | bytes 1572872 | tf_op jit(solution)/shard_map/ppermute | solution.py:48
  67.0 24.0 %collective-permute-start.10 = (bf16[512,512]{1,0:T(8,128)(2,1)}, bf16[512,512]{1,0:T(8,128)(2,1)}, u32[]{:S(2)}, u32[]{:S(2)}) collective-permute-start(bf16[512,512]{1,0:T(8,128)(2,1)} %collective-permute-done.8), channel_id=1, source_target_pairs={{0,1},{1,2},{2,3},{3,4},{4,5},{5,6},{6,7},{7,8},{8,9},{9,10},{10,1... | collective-permute-start | bytes 1572872 | tf_op jit(solution)/shard_map/ppermute | solution.py:43
  89.0 11.4 %collective-permute-start.11 = (bf16[512,512]{1,0:T(8,128)(2,1)}, bf16[512,512]{1,0:T(8,128)(2,1)S(1)}, u32[]{:S(2)}, u32[]{:S(2)}) collective-permute-start(bf16[512,512]{1,0:T(8,128)(2,1)} %collective-permute-done.9), channel_id=1, source_target_pairs={{0,15},{1,0},{2,1},{3,2},{4,3},{5,4},{6,5},{7,6},{8,7},{9,8},{10,9... | collective-permute-start | bytes 1572872 | tf_op jit(solution)/shard_map/ppermute | solution.py:48
  91.0 14.3 %collective-permute-start.12 = (bf16[512,512]{1,0:T(8,128)(2,1)}, bf16[512,512]{1,0:T(8,128)(2,1)S(1)}, u32[]{:S(2)}, u32[]{:S(2)}) collective-permute-start(bf16[512,512]{1,0:T(8,128)(2,1)} %collective-permute-done.10), channel_id=1, source_target_pairs={{0,1},{1,2},{2,3},{3,4},{4,5},{5,6},{6,7},{7,8},{8,9},{9,10},{10,1... | collective-permute-start | bytes 1572872 | tf_op jit(solution)/shard_map/ppermute | solution.py:43
  100.4 12.9 %collective-permute-start.13 = (bf16[512,512]{1,0:T(8,128)(2,1)S(1)}, bf16[512,512]{1,0:T(8,128)(2,1)S(1)}, u32[]{:S(2)}, u32[]{:S(2)}) collective-permute-start(bf16[512,512]{1,0:T(8,128)(2,1)S(1)} %collective-permute-done.11), channel_id=1, source_target_pairs={{0,15},{1,0},{2,1},{3,2},{4,3},{5,4},{6,5},{7,6},{8,7},{9,8},{10,9... | collective-permute-start | bytes 1572872 | tf_op jit(solution)/shard_map/ppermute | solution.py:48
  105.3 12.4 %collective-permute-start.14 = (bf16[512,512]{1,0:T(8,128)(2,1)S(1)}, bf16[512,512]{1,0:T(8,128)(2,1)S(1)}, u32[]{:S(2)}, u32[]{:S(2)}) collective-permute-start(bf16[512,512]{1,0:T(8,128)(2,1)S(1)} %collective-permute-done.12), channel_id=1, source_target_pairs={{0,1},{1,2},{2,3},{3,4},{4,5},{5,6},{6,7},{7,8},{8,9},{9,10},{10,1... | collective-permute-start | bytes 1572872 | tf_op jit(solution)/shard_map/ppermute | solution.py:43
  118.5 6.6 %copy-start.7 = (u32[32]{0:T(128)S(1)}, u32[32]{0:T(128)}, u32[]{:S(2)}) copy-start(u32[32]{0:T(128)} %constant.147) | copy-start | bytes 388
  118.5 7.8 %copy-start.6 = (s32[2]{0:T(128)S(1)}, s32[2]{0:T(128)}, u32[]{:S(2)}) copy-start(s32[2]{0:T(128)} %param.17) | copy-start | bytes 28
  118.5 51.5 %copy-start.2 = (bf16[128,4096]{1,0:T(8,128)(2,1)S(1)}, bf16[128,4096]{1,0:T(8,128)(2,1)}, u32[]{:S(2)}) copy-start(bf16[128,4096]{1,0:T(8,128)(2,1)} %param.12) | copy-start | bytes 3145732
  170.3 4.6 %copy-start.4 = (bf16[2048,4,128]{0,2,1:T(8,128)(2,1)S(1)}, bf16[2048,4,128]{0,2,1:T(8,128)(2,1)}, u32[]{:S(2)}) copy-start(bf16[2048,4,128]{0,2,1:T(8,128)(2,1)} %get-tuple-element.63) | copy-start | bytes 6291460 | tf_op jit(solution)/shard_map/cond
  185.4 4.6 %copy-start.5 = (bf16[2048,4,128]{0,2,1:T(8,128)(2,1)S(1)}, bf16[2048,4,128]{0,2,1:T(8,128)(2,1)}, u32[]{:S(2)}) copy-start(bf16[2048,4,128]{0,2,1:T(8,128)(2,1)} %get-tuple-element.68) | copy-start | bytes 6291460 | tf_op jit(solution)/shard_map/cond
  (1 other events, 3.2 us)
Sparse Core Ops, SparseCore 0:
  51.1 50.1 all-gather.2
  125.1 44.7 all-gather.4
